TPU v7x, 128 devices: a whole 4x4x4 slice. The times are simulated.
128 devices in a mesh: row: 8 (over x_lo, z), col: 16 (over x_hi, y, core).
Axes of the slice: x: 4 (x_hi: 2, x_lo: 2; x = x_hi * 2 + x_lo), y: 4, z: 4, core: 2. Of those that a mesh axis runs over, the one named last changes fastest.
Arguments:
- level_set: float32 [384, 384, 384], P('col', 'row'), may hold values from -7 to 7
- image: float32 [384, 384, 384], P('col', 'row'), may hold values from -6 to 6
Outputs:
- updated_level: float32 [384, 384, 384], P('col', 'row')
All inputs are finite; a program needn't handle non-finite values.
Results may differ from a plain program's by a relative error of at most 0.00021.
Values sent between devices are 32-bit elements; how exact they have to be, the bound alone decides.
A program may use at most 128 MiB of HBM per device.

v0:
```python
import jax
import jax.numpy as jnp
from jax import lax
from jax.sharding import PartitionSpec as P

RADIUS = 6
sigma_cells = 8.0
dt_step = 0.5
nu_diff = 0.1
eps_fit = 0.05


def extended(value, sides, width):
    for axis, dim in sides:
        devices, length = (lax.axis_size(axis), value.shape[dim])
        up = [(i, (i + 1) % devices) for i in range(devices)]
        down = [(j, i) for i, j in up]
        last = lax.slice_in_dim(value, length - width, length, axis=dim)
        first = lax.slice_in_dim(value, 0, width, axis=dim)
        before = lax.ppermute(last, axis, up)
        after = lax.ppermute(first, axis, down)
        value = jnp.concatenate([before, value, after], axis=dim)
    return value


def tap_weight(offset):
    tap_offsets = lax.iota(jnp.int32, 2 * RADIUS + 1) - RADIUS
    tap_float = tap_offsets.astype(jnp.float32)
    total_weight = jnp.sum(jnp.exp(-tap_float * tap_float / (2.0 * sigma_cells * sigma_cells)))
    off_float = offset.astype(jnp.float32)
    inside = jnp.abs(offset) <= RADIUS
    weights = jnp.where(
        inside, jnp.exp(-off_float * off_float / (2.0 * sigma_cells * sigma_cells)), 0.0
    )
    return weights / total_weight


def gauss_table(length):
    indices = lax.iota(jnp.int32, length)
    distance = jnp.abs(indices[:, None] - indices[None, :])
    distance = jnp.minimum(distance, length - distance)
    return tap_weight(distance)


def lines_along_x(fields, kernel_table):
    along_x = jnp.einsum("fzyx,xw->fwzy", fields, kernel_table, precision=lax.Precision.HIGHEST)
    return along_x.reshape(4, fields.shape[3], fields.shape[1] * fields.shape[2])


def fit_coeffs(smoothed):
    first, second, third, fourth = (smoothed[0], smoothed[1], smoothed[2], smoothed[3])
    inside_mean = first / (second + eps_fit)
    outside_mean = (third - first) / (1.0 - second + eps_fit)
    spread = fourth - third * third + eps_fit
    slope_term = 2.0 * (inside_mean - outside_mean) / spread
    offset = (outside_mean * outside_mean - inside_mean * inside_mean) / spread
    return jnp.stack([slope_term, offset])


def body(level_set, image):
    highest = lax.Precision.HIGHEST
    z_local, y_local, length = level_set.shape
    n_row = lax.axis_size("row")
    kernel_table = gauss_table(length)
    heaviside = 0.5 + jnp.arctan(level_set) / jnp.pi
    fields = jnp.stack([heaviside * image, heaviside, image, image * image])
    along_x = lines_along_x(fields, kernel_table)
    row_table = kernel_table.reshape(n_row, y_local, length)
    x_local = length // n_row
    received = lax.all_to_all(along_x, "row", split_axis=1, concat_axis=2, tiled=True)
    received = received.reshape(4, x_local, n_row, z_local, y_local)
    along_y = jnp.einsum("fwrzy,ryv->fwzv", received, row_table, precision=highest)
    received_z = lax.all_to_all(along_y, "col", split_axis=3, concat_axis=2, tiled=True)
    along_z = jnp.einsum("fxzy,zw->fxyw", received_z, kernel_table, precision=highest)
    coeffs = fit_coeffs(along_z)
    returned = lax.all_to_all(coeffs, "col", split_axis=3, concat_axis=2, tiled=True)
    returned = lax.all_to_all(returned, "row", split_axis=2, concat_axis=1, tiled=True)
    local_coeffs = jnp.transpose(returned, (0, 3, 2, 1))
    forcing = image * local_coeffs[0] + local_coeffs[1]
    padded = extended(level_set, (("row", 1), ("col", 0)), 1)
    laplace = (
        padded[2:, 1:-1, :]
        + padded[:-2, 1:-1, :]
        + padded[1:-1, 2:, :]
        + padded[1:-1, :-2, :]
        + jnp.roll(level_set, 1, 2)
        + jnp.roll(level_set, -1, 2)
        - 6.0 * level_set
    )
    dirac_weight = 1.0 / (jnp.pi * (1.0 + level_set * level_set))
    return level_set + dt_step * (nu_diff * laplace + dirac_weight * forcing)


def solution(mesh):
    return jax.shard_map(
        body,
        mesh=mesh,
        in_specs=(P("col", "row", None), P("col", "row", None)),
        out_specs=P("col", "row", None),
        check_vma=False,
    )
```

profile of v0, /device:TPU:25, one launch (start us, length us, event | category | flops | bytes accessed | tf_op | source)
XLA Modules:
  0.0 704.8 jit_solution(235425075818692739)
XLA Ops:
  4.9 16.5 %fusion = f32[384,4,24,48]{0,3,2,1:T(8,128)} fusion(f32[1,24,48,384]{3,2,1,0:T(8,128)S(1)} %get-tuple-element.17, f32[1,24,48,384]{3,2,1,0:T(8,128)S(1)} %bitcast.87, f32[1,24,48,384]{3,2,1,0:T(8,128)S(1)} %get-tuple-element.16, f32[1,24,48,384]{3,2,1,0:T(8,128)S(1)} %get-tuple-element.15, f32[]{:T(128)} %fusion.59), kind=kOutput, calls=%fused_computation | convolution fusion | flops 8160804864 | bytes 14155780 | tf_op jit(solution)/shard_map/fzyx,xw->fwzy/dot_general | solution.py:46
  21.4 10.1 %copy.27 = f32[4,384,1152]{2,0,1:T(4,128)} copy(f32[4,384,1152]{1,2,0:T(8,128)} %bitcast.86) | data formatting | bytes 14155776 | tf_op jit(solution)/shard_map/reshape | solution.py:47
  38.0 79.6 %all-to-all-done = f32[4,384,1152]{2,0,1:T(4,128)} async-done(((f32[4,384,1152]{2,0,1:T(4,128)}), f32[4,384,1152]{2,0,1:T(4,128)}, u32[]{:S(2)}, u32[]{:S(2)}) %all-to-all-start) | async-done | bytes 7077920 | tf_op jit(solution)/shard_map/all_to_all | solution.py:70
  126.1 15.1 %reshape.71 = f32[4,48,8,24,48]{4,3,2,1,0:T(8,128)} reshape(f32[4,48,8,1152]{3,2,1,0:T(8,128)} %copy.29) | data formatting | bytes 14155776 | tf_op jit(solution)/shard_map/reshape | solution.py:71
  141.2 22.0 %convolution_bitcast_fusion = f32[4,48,24,384]{3,2,1,0:T(8,128)} fusion(f32[4,48,8,24,48]{4,3,2,1,0:T(8,128)} %reshape.71, f32[]{:T(128)} %fusion.59, s32[8,48]{1,0:T(8,128)S(1)} %multiply_add_fusion.1), kind=kOutput, calls=%fused_computation.9 | convolution fusion | flops 8155496448 | bytes 14157316 | tf_op jit(solution)/shard_map/fwrzy,ryv->fwzv/dot_general | solution.py:72
  163.2 17.4 %copy.30 = f32[4,48,24,384]{1,2,0,3:T(8,128)} copy(f32[4,48,24,384]{3,2,1,0:T(8,128)} %convolution_bitcast_fusion) | data formatting | bytes 14155776 | tf_op jit(solution)/shard_map/fwrzy,ryv->fwzv/dot_general | solution.py:72
  180.6 22.5 %reshape.75 = f32[16,1,110592]{2,1,0:T(1,128)} reshape(f32[384,4,24,48]{3,2,1,0:T(8,128)} %bitcast.76) | data formatting | bytes 14155776
  203.1 88.3 %all_to_all.69 = f32[16,1,110592]{2,1,0:T(1,128)} all-to-all(f32[16,1,110592]{2,1,0:T(1,128)} %reshape.75), channel_id=1, replica_groups=mesh['row'=8,'col'=16] {'col'}, dimensions={0} | all-to-all | bytes 14155776 | tf_op jit(solution)/shard_map/all_to_all | solution.py:73
  292.0 76.7 %reduce = f32[16,110592]{1,0:T(8,128)} reduce(f32[16,1,110592]{2,1,0:T(1,128)} %all_to_all.69, f32[]{:T(128)} %broadcast.153), dimensions={1}, to_apply=%all_to_all.53.reduce_sub_computation | reduce | bytes 14155780 | tf_op jit(solution)/shard_map/all_to_all | solution.py:73
  368.7 18.8 %reshape.76 = f32[384,4,24,48]{3,2,1,0:T(8,128)} reshape(f32[16,110592]{1,0:T(8,128)} %reduce) | data formatting | bytes 14155776
  387.5 15.8 %copy.32 = f32[4,48,16,24,24]{1,4,3,2,0:T(8,128)} copy(f32[4,48,16,24,24]{1,3,0,4,2:T(8,128)} %bitcast.77) | data formatting | bytes 14155776 | tf_op jit(solution)/shard_map/all_to_all | solution.py:73
  403.3 14.5 %copy.33 = f32[4,48,384,24]{2,3,1,0:T(8,128)} copy(f32[4,48,384,24]{1,3,2,0:T(8,128)} %bitcast.78) | data formatting | bytes 14155776 | tf_op jit(solution)/shard_map/all_to_all | solution.py:73
  417.8 19.2 %fusion.38 = f32[4,48,24,384]{3,2,1,0:T(8,128)S(1)} fusion(f32[4,48,384,24]{2,3,1,0:T(8,128)} %copy.33, f32[]{:T(128)} %fusion.59), kind=kOutput, calls=%fused_computation.63 | convolution fusion | flops 8155496448 | bytes 14155780 | tf_op jit(solution)/shard_map/fxzy,zw->fxyw/dot_general | solution.py:74
  444.1 15.2 %reshape.77 = f32[16,1,55296]{2,1,0:T(1,128)} reshape(f32[384,2,24,48]{3,2,1,0:T(8,128)} %bitcast.79) | data formatting | bytes 7077888
  459.3 48.5 %all_to_all.70 = f32[16,1,55296]{2,1,0:T(1,128)S(1)} all-to-all(f32[16,1,55296]{2,1,0:T(1,128)} %reshape.77), channel_id=1, replica_groups=mesh['row'=8,'col'=16] {'col'}, dimensions={0} | all-to-all | bytes 7077888 | tf_op jit(solution)/shard_map/all_to_all | solution.py:76
  507.8 30.2 %reduce.1 = f32[16,55296]{1,0:T(8,128)} reduce(f32[16,1,55296]{2,1,0:T(1,128)S(1)} %all_to_all.70, f32[]{:T(128)} %broadcast.153), dimensions={1}, to_apply=%all_to_all.57.reduce_sub_computation | reduce | bytes 7077892 | tf_op jit(solution)/shard_map/all_to_all | solution.py:76
  538.0 11.1 %reshape.78 = f32[384,2,24,48]{3,2,1,0:T(8,128)} reshape(f32[16,55296]{1,0:T(8,128)} %reduce.1) | data formatting | bytes 7077888
  549.1 6.7 copy.36
  560.2 12.1 %reshape.79 = f32[8,1,110592]{2,1,0:T(1,128)} reshape(f32[384,2,24,48]{3,2,1,0:T(8,128)} %bitcast.82) | data formatting | bytes 7077888
  582.4 37.7 %collective-permute-done = f32[24,1,384]{2,1,0:T(1,128)S(1)} collective-permute-done((f32[24,1,384]{2,1,0:T(1,128)S(1)}, f32[24,1,384]{2,1,0:T(1,128)S(1)}, u32[]{:S(2)}, u32[]{:S(2)}) %collective-permute-start) | collective-permute-done | bytes 36896 | tf_op jit(solution)/shard_map/ppermute | solution.py:20
  628.0 39.6 %reduce.2 = f32[8,110592]{1,0:T(8,128)} reduce(f32[8,1,110592]{2,1,0:T(1,128)} %all-to-all-done.3, f32[]{:T(128)} %broadcast.153), dimensions={1}, to_apply=%all_to_all.61.reduce_sub_computation | reduce | bytes 7077892 | tf_op jit(solution)/shard_map/all_to_all | solution.py:77
  667.6 9.4 %reshape.80 = f32[384,2,24,48]{3,2,1,0:T(8,128)} reshape(f32[8,110592]{1,0:T(8,128)} %reduce.2) | data formatting | bytes 7077888
  677.0 12.8 %copy.39 = f32[2,8,48,48,24]{2,1,3,4,0:T(8,128)} copy(f32[2,8,48,48,24]{2,4,0,3,1:T(8,128)} %bitcast.83) | data formatting | bytes 7077888 | tf_op jit(solution)/shard_map/all_to_all | solution.py:77
  689.8 8.3 %all_to_all.64 = f32[2,384,48,24]{1,2,3,0:T(8,128)} reshape(f32[2,8,48,48,24]{2,1,3,4,0:T(8,128)} %copy.39) | data formatting | bytes 7077888 | tf_op jit(solution)/shard_map/all_to_all | solution.py:77
  (33 shorter events, 56.2 us)
Async XLA Ops:
  0.6 4.3 copy-start.1
  31.5 86.1 %all-to-all-start = ((f32[4,384,1152]{2,0,1:T(4,128)}), f32[4,384,1152]{2,0,1:T(4,128)}, u32[]{:S(2)}, u32[]{:S(2)}) async-start(f32[4,384,1152]{2,0,1:T(4,128)} %copy.27), calls=%async_computation | async-start | bytes 14155776 | tf_op jit(solution)/shard_map/all_to_all | solution.py:70
  572.3 4.6 copy-start
  572.3 55.6 %all-to-all-start.3 = ((f32[8,1,110592]{2,1,0:T(1,128)}), f32[8,1,110592]{2,1,0:T(1,128)}, u32[]{:S(2)}, u32[]{:S(2)}) async-start(f32[8,1,110592]{2,1,0:T(1,128)} %reshape.79), calls=%async_computation.3 | async-start | bytes 7077888 | tf_op jit(solution)/shard_map/all_to_all | solution.py:77
  577.0 43.1 %collective-permute-start = (f32[24,1,384]{2,1,0:T(1,128)S(1)}, f32[24,1,384]{2,1,0:T(1,128)S(1)}, u32[]{:S(2)}, u32[]{:S(2)}) collective-permute-start(f32[24,1,384]{2,1,0:T(1,128)S(1)} %get-tuple-element.14), channel_id=1, source_target_pairs={{0,16},{16,32},{32,48},{48,64},{64,80},{80,96},{96,112},{112,0},{1... | collective-permute-start | bytes 110600 | tf_op jit(solution)/shard_map/ppermute | solution.py:20
  578.4 41.7 %collective-permute-start.1 = (f32[24,1,384]{2,1,0:T(1,128)S(1)}, f32[24,1,384]{2,1,0:T(1,128)S(1)}, u32[]{:S(2)}, u32[]{:S(2)}) collective-permute-start(f32[24,1,384]{2,1,0:T(1,128)S(1)} %get-tuple-element.13), channel_id=1, source_target_pairs={{16,0},{32,16},{48,32},{64,48},{80,64},{96,80},{112,96},{0,112},{1... | collective-permute-start | bytes 110600 | tf_op jit(solution)/shard_map/ppermute | solution.py:21
  620.1 0.6 copy-start.2
  620.7 0.7 copy-start.3
  621.4 76.7 %collective-permute-start.2 = (f32[1,50,384]{2,1,0:T(8,128)}, f32[1,50,384]{2,1,0:T(8,128)}, u32[]{:S(2)}, u32[]{:S(2)}) collective-permute-start(f32[1,50,384]{2,1,0:T(8,128)} %get-tuple-element.7), channel_id=1, source_target_pairs={{1,0},{2,1},{3,2},{4,3},{5,4},{6,5},{7,6},{8,7},{9,8},{10,9},{11,1... | collective-permute-start | bytes 230408 | tf_op jit(solution)/shard_map/ppermute | solution.py:21
  622.7 75.4 %collective-permute-start.3 = (f32[1,50,384]{2,1,0:T(8,128)}, f32[1,50,384]{2,1,0:T(8,128)}, u32[]{:S(2)}, u32[]{:S(2)}) collective-permute-start(f32[1,50,384]{2,1,0:T(8,128)} %get-tuple-element.8), channel_id=1, source_target_pairs={{0,1},{1,2},{2,3},{3,4},{4,5},{5,6},{6,7},{7,8},{8,9},{9,10},{10,1... | collective-permute-start | bytes 230408 | tf_op jit(solution)/shard_map/ppermute | solution.py:20
where the time goes:
time: 715 us; the launch traced here: 705 us
  local copies, waits for them, and re-layouts  213 us (30%)
  other arithmetic  160 us (22%)
  blocking collectives  137 us (19%)
  waiting for transfers between devices  117 us (16%)
  matrix products  57.7 us (8%)
  starting transfers between devices  20.1 us (3%)
    unnamed x14, local copies, waits for them, and re-layouts  89.8 us
    all_to_all x1, blocking collectives, body(): lax.all_to_all(along_y, 'col', split_axis=3, concat_axis=2, tiled=True)  88.3 us
    all_to_all x1, waiting for transfers between devices, body(): lax.all_to_all(along_x, 'row', split_axis=1, concat_axis=2, tiled=True)  79.6 us
    all_to_all x1, other arithmetic, body(): lax.all_to_all(along_y, 'col', split_axis=3, concat_axis=2, tiled=True)  76.7 us
    all_to_all x1, blocking collectives, body(): lax.all_to_all(coeffs, 'col', split_axis=3, concat_axis=2, tiled=True)  48.5 us
    all_to_all x1, other arithmetic, body(): lax.all_to_all(returned, 'row', split_axis=2, concat_axis=1, tiled=True)  39.6 us
    ppermute x2, waiting for transfers between devices, extended(): before = lax.ppermute(last, axis, up)  37.7 us
    all_to_all x3, local copies, waits for them, and re-layouts, body(): lax.all_to_all(along_y, 'col', split_axis=3, concat_axis=2, tiled=True)  30.8 us
  transfers between devices with their start and end apart: 6, of which 2 were waited for; matrix products, arithmetic and copies ran while one was open for 9% of the time, Pallas kernels for 0%

commit v1 on v0

--- a/solution.py
+++ b/solution.py
@@ -70,7 +70,10 @@
     received = lax.all_to_all(along_x, "row", split_axis=1, concat_axis=2, tiled=True)
     received = received.reshape(4, x_local, n_row, z_local, y_local)
     along_y = jnp.einsum("fwrzy,ryv->fwzv", received, row_table, precision=highest)
-    received_z = lax.all_to_all(along_y, "col", split_axis=3, concat_axis=2, tiled=True)
+    received_z = jnp.concatenate(
+        lax.all_to_all(jnp.stack(jnp.split(along_y, lax.axis_size("col"), axis=3)), "col", 0, 0),
+        axis=2,
+    )
     along_z = jnp.einsum("fxzy,zw->fxyw", received_z, kernel_table, precision=highest)
     coeffs = fit_coeffs(along_z)
     returned = lax.all_to_all(coeffs, "col", split_axis=3, concat_axis=2, tiled=True)

time: 715 us -> 759 us (1.062)
  local copies, waits for them, and re-layouts: 213 us -> 257 us
    another operation x0 -> x2, local copies, waits for them, and re-layouts: none -> 32.5 us  [body(): jnp.stack(jnp.split(along_y, lax.axis_size('col'), axis=3))]
    unnamed x14 -> x29, local copies, waits for them, and re-layouts: 89.8 us -> 121 us
    all_to_all x3 -> x1, local copies, waits for them, and re-layouts: 30.8 us -> 0.59 us  [body(): lax.all_to_all(jnp.stack(jnp.split(along_y, lax.axis_size('col'), axis=3)...]
    reshape x0 -> x3, local copies, waits for them, and re-layouts: none -> 28.6 us  [body(): jnp.concatenate(lax.all_to_all(jnp.stack(jnp.split(along_y, lax.axis_size...]
    dot_general x1 -> x0, local copies, waits for them, and re-layouts: 17.4 us -> none  [body(): jnp.einsum('fwrzy,ryv->fwzv', received, row_table, precision=highest)]
where the time goes in v1:
time: 759 us; the launch traced here: 749 us
  local copies, waits for them, and re-layouts  257 us (34%)
  other arithmetic  160 us (21%)
  blocking collectives  137 us (18%)
  waiting for transfers between devices  117 us (15%)
  matrix products  57.5 us (8%)
  starting transfers between devices  19.8 us (3%)
    unnamed x29, local copies, waits for them, and re-layouts  121 us
    all_to_all x1, blocking collectives, body(): lax.all_to_all(jnp.stack(jnp.split(along_y, lax.axis_size('col'), axis=3)...  88.3 us
    all_to_all x1, waiting for transfers between devices, body(): lax.all_to_all(along_x, 'row', split_axis=1, concat_axis=2, tiled=True)  79.6 us
    all_to_all x1, other arithmetic, body(): lax.all_to_all(jnp.stack(jnp.split(along_y, lax.axis_size('col'), axis=3)...  76.7 us
    all_to_all x1, blocking collectives, body(): lax.all_to_all(coeffs, 'col', split_axis=3, concat_axis=2, tiled=True)  48.5 us
    all_to_all x1, other arithmetic, body(): lax.all_to_all(returned, 'row', split_axis=2, concat_axis=1, tiled=True)  39.6 us
    ppermute x2, waiting for transfers between devices, extended(): before = lax.ppermute(last, axis, up)  37.7 us
    another operation x2, local copies, waits for them, and re-layouts, body(): jnp.stack(jnp.split(along_y, lax.axis_size('col'), axis=3))  32.5 us
  transfers between devices with their start and end apart: 6, of which 2 were waited for; matrix products, arithmetic and copies ran while one was open for 9% of the time, Pallas kernels for 0%

profile of v1, /device:TPU:25, one launch (start us, length us, event | category | flops | bytes accessed | tf_op | source)
XLA Modules:
  0.0 748.7 jit_solution(17188797253840994411)
XLA Ops:
  4.9 16.5 %fusion = f32[384,4,24,48]{0,3,2,1:T(8,128)} fusion(f32[1,24,48,384]{3,2,1,0:T(8,128)S(1)} %get-tuple-element.17, f32[1,24,48,384]{3,2,1,0:T(8,128)S(1)} %bitcast.150, f32[1,24,48,384]{3,2,1,0:T(8,128)S(1)} %get-tuple-element.16, f32[1,24,48,384]{3,2,1,0:T(8,128)S(1)} %get-tuple-element.15, f32[]{:T(128)} %fusion.75), kind=kOutput, calls=%fused_computation | convolution fusion | flops 8160804864 | bytes 14155780 | tf_op jit(solution)/shard_map/fzyx,xw->fwzy/dot_general | solution.py:46
  21.4 10.1 %copy.24 = f32[4,384,1152]{2,0,1:T(4,128)} copy(f32[4,384,1152]{1,2,0:T(8,128)} %bitcast.149) | data formatting | bytes 14155776 | tf_op jit(solution)/shard_map/reshape | solution.py:47
  37.7 79.6 %all-to-all-done = f32[4,384,1152]{2,0,1:T(4,128)} async-done(((f32[4,384,1152]{2,0,1:T(4,128)}), f32[4,384,1152]{2,0,1:T(4,128)}, u32[]{:S(2)}, u32[]{:S(2)}) %all-to-all-start) | async-done | bytes 7077920 | tf_op jit(solution)/shard_map/all_to_all | solution.py:70
  125.9 15.1 %reshape.77 = f32[4,48,8,24,48]{4,3,2,1,0:T(8,128)} reshape(f32[4,48,8,1152]{3,2,1,0:T(8,128)} %copy.26) | data formatting | bytes 14155776 | tf_op jit(solution)/shard_map/reshape | solution.py:71
  140.9 21.7 %convolution_bitcast_fusion = f32[4,48,24,384]{3,2,1,0:T(8,128)S(1)} fusion(f32[4,48,8,24,48]{4,3,2,1,0:T(8,128)} %reshape.77, f32[]{:T(128)} %fusion.75, s32[8,48]{1,0:T(8,128)S(1)} %multiply_add_fusion.1), kind=kOutput, calls=%fused_computation.9 | convolution fusion | flops 8155496448 | bytes 14157316 | tf_op jit(solution)/shard_map/fwrzy,ryv->fwzv/dot_general | solution.py:72
  195.9 30.4 %copy.27 = f32[16,4,48,24,24]{2,4,3,1,0:T(8,128)} copy(f32[16,4,48,24,24]{4,3,2,1,0:T(8,128)} %fusion.8) | data formatting | bytes 14155776 | tf_op jit(solution)/shard_map/stack | solution.py:74
  226.2 22.5 %reshape.83 = f32[16,1,110592]{2,1,0:T(1,128)} reshape(f32[16,4,24,24,48]{4,3,2,1,0:T(8,128)} %bitcast.140) | data formatting | bytes 14155776
  248.7 88.3 %all_to_all.56 = f32[16,1,110592]{2,1,0:T(1,128)} all-to-all(f32[16,1,110592]{2,1,0:T(1,128)} %reshape.83), channel_id=1, replica_groups=mesh['row'=8,'col'=16] {'col'}, dimensions={0} | all-to-all | bytes 14155776 | tf_op jit(solution)/shard_map/all_to_all | solution.py:74
  337.6 76.7 %reduce = f32[16,110592]{1,0:T(8,128)} reduce(f32[16,1,110592]{2,1,0:T(1,128)} %all_to_all.56, f32[]{:T(128)} %broadcast.153), dimensions={1}, to_apply=%all_to_all.43.reduce_sub_computation | reduce | bytes 14155780 | tf_op jit(solution)/shard_map/all_to_all | solution.py:74
  414.2 18.8 %reshape.84 = f32[16,4,24,24,48]{4,3,2,1,0:T(8,128)} reshape(f32[16,110592]{1,0:T(8,128)} %reduce) | data formatting | bytes 14155776
  433.1 7.3 bitcast_bitcast_fusion
  440.4 6.9 copy.28
  447.3 14.4 %copy.29 = f32[4,48,384,24]{2,3,1,0:T(8,128)} copy(f32[4,48,384,24]{1,3,2,0:T(8,128)} %bitcast.141) | data formatting | bytes 14155776 | tf_op jit(solution)/shard_map/reshape | solution.py:73
  461.7 19.2 %fusion.54 = f32[4,48,24,384]{3,2,1,0:T(8,128)S(1)} fusion(f32[4,48,384,24]{2,3,1,0:T(8,128)} %copy.29, f32[]{:T(128)} %fusion.75), kind=kOutput, calls=%fused_computation.95 | convolution fusion | flops 8155496448 | bytes 14155780 | tf_op jit(solution)/shard_map/fxzy,zw->fxyw/dot_general | solution.py:77
  488.0 15.2 %reshape.85 = f32[16,1,55296]{2,1,0:T(1,128)} reshape(f32[384,2,24,48]{3,2,1,0:T(8,128)} %bitcast.142) | data formatting | bytes 7077888
  503.2 48.5 %all_to_all.57 = f32[16,1,55296]{2,1,0:T(1,128)S(1)} all-to-all(f32[16,1,55296]{2,1,0:T(1,128)} %reshape.85), channel_id=1, replica_groups=mesh['row'=8,'col'=16] {'col'}, dimensions={0} | all-to-all | bytes 7077888 | tf_op jit(solution)/shard_map/all_to_all | solution.py:79
  551.7 30.2 %reduce.1 = f32[16,55296]{1,0:T(8,128)} reduce(f32[16,1,55296]{2,1,0:T(1,128)S(1)} %all_to_all.57, f32[]{:T(128)} %broadcast.153), dimensions={1}, to_apply=%all_to_all.44.reduce_sub_computation | reduce | bytes 7077892 | tf_op jit(solution)/shard_map/all_to_all | solution.py:79
  581.9 11.1 %reshape.86 = f32[384,2,24,48]{3,2,1,0:T(8,128)} reshape(f32[16,55296]{1,0:T(8,128)} %reduce.1) | data formatting | bytes 7077888
  604.1 12.1 %reshape.87 = f32[8,1,110592]{2,1,0:T(1,128)} reshape(f32[384,2,24,48]{3,2,1,0:T(8,128)} %bitcast.145) | data formatting | bytes 7077888
  626.4 37.7 %collective-permute-done = f32[24,1,384]{2,1,0:T(1,128)S(1)} collective-permute-done((f32[24,1,384]{2,1,0:T(1,128)S(1)}, f32[24,1,384]{2,1,0:T(1,128)S(1)}, u32[]{:S(2)}, u32[]{:S(2)}) %collective-permute-start) | collective-permute-done | bytes 36896 | tf_op jit(solution)/shard_map/ppermute | solution.py:20
  671.9 39.6 %reduce.2 = f32[8,110592]{1,0:T(8,128)} reduce(f32[8,1,110592]{2,1,0:T(1,128)} %all-to-all-done.3, f32[]{:T(128)} %broadcast.153), dimensions={1}, to_apply=%all_to_all.48.reduce_sub_computation | reduce | bytes 7077892 | tf_op jit(solution)/shard_map/all_to_all | solution.py:80
  711.5 9.4 %reshape.88 = f32[384,2,24,48]{3,2,1,0:T(8,128)} reshape(f32[8,110592]{1,0:T(8,128)} %reduce.2) | data formatting | bytes 7077888
  720.9 12.8 %copy.35 = f32[2,8,48,48,24]{2,1,3,4,0:T(8,128)} copy(f32[2,8,48,48,24]{2,4,0,3,1:T(8,128)} %bitcast.146) | data formatting | bytes 7077888 | tf_op jit(solution)/shard_map/all_to_all | solution.py:80
  733.7 8.3 %all_to_all.51 = f32[2,384,48,24]{1,2,3,0:T(8,128)} reshape(f32[2,8,48,48,24]{2,1,3,4,0:T(8,128)} %copy.35) | data formatting | bytes 7077888 | tf_op jit(solution)/shard_map/all_to_all | solution.py:80
  (50 shorter events, 95.8 us)
Async XLA Ops:
  0.6 4.3 copy-start.1
  31.5 85.8 %all-to-all-start = ((f32[4,384,1152]{2,0,1:T(4,128)}), f32[4,384,1152]{2,0,1:T(4,128)}, u32[]{:S(2)}, u32[]{:S(2)}) async-start(f32[4,384,1152]{2,0,1:T(4,128)} %copy.24), calls=%async_computation | async-start | bytes 14155776 | tf_op jit(solution)/shard_map/all_to_all | solution.py:70
  616.2 4.6 copy-start
  616.2 55.6 %all-to-all-start.3 = ((f32[8,1,110592]{2,1,0:T(1,128)}), f32[8,1,110592]{2,1,0:T(1,128)}, u32[]{:S(2)}, u32[]{:S(2)}) async-start(f32[8,1,110592]{2,1,0:T(1,128)} %reshape.87), calls=%async_computation.3 | async-start | bytes 7077888 | tf_op jit(solution)/shard_map/all_to_all | solution.py:80
  620.9 43.1 %collective-permute-start = (f32[24,1,384]{2,1,0:T(1,128)S(1)}, f32[24,1,384]{2,1,0:T(1,128)S(1)}, u32[]{:S(2)}, u32[]{:S(2)}) collective-permute-start(f32[24,1,384]{2,1,0:T(1,128)S(1)} %get-tuple-element.14), channel_id=1, source_target_pairs={{0,16},{16,32},{32,48},{48,64},{64,80},{80,96},{96,112},{112,0},{1... | collective-permute-start | bytes 110600 | tf_op jit(solution)/shard_map/ppermute | solution.py:20
  622.3 41.7 %collective-permute-start.1 = (f32[24,1,384]{2,1,0:T(1,128)S(1)}, f32[24,1,384]{2,1,0:T(1,128)S(1)}, u32[]{:S(2)}, u32[]{:S(2)}) collective-permute-start(f32[24,1,384]{2,1,0:T(1,128)S(1)} %get-tuple-element.13), channel_id=1, source_target_pairs={{16,0},{32,16},{48,32},{64,48},{80,64},{96,80},{112,96},{0,112},{1... | collective-permute-start | bytes 110600 | tf_op jit(solution)/shard_map/ppermute | solution.py:21
  664.0 0.6 copy-start.2
  664.6 0.7 copy-start.3
  665.3 76.7 %collective-permute-start.2 = (f32[1,50,384]{2,1,0:T(8,128)}, f32[1,50,384]{2,1,0:T(8,128)}, u32[]{:S(2)}, u32[]{:S(2)}) collective-permute-start(f32[1,50,384]{2,1,0:T(8,128)} %get-tuple-element.7), channel_id=1, source_target_pairs={{1,0},{2,1},{3,2},{4,3},{5,4},{6,5},{7,6},{8,7},{9,8},{10,9},{11,1... | collective-permute-start | bytes 230408 | tf_op jit(solution)/shard_map/ppermute | solution.py:21
  666.6 75.4 %collective-permute-start.3 = (f32[1,50,384]{2,1,0:T(8,128)}, f32[1,50,384]{2,1,0:T(8,128)}, u32[]{:S(2)}, u32[]{:S(2)}) collective-permute-start(f32[1,50,384]{2,1,0:T(8,128)} %get-tuple-element.8), channel_id=1, source_target_pairs={{0,1},{1,2},{2,3},{3,4},{4,5},{5,6},{6,7},{7,8},{8,9},{9,10},{10,1... | collective-permute-start | bytes 230408 | tf_op jit(solution)/shard_map/ppermute | solution.py:20
